TPU v7x, 32 devices: a whole 2x2x4 slice. The times are simulated.
32 devices in a mesh: dp: 2 (over z_hi), expert: 8 (over y, x, core), tensor: 2 (over z_lo).
Axes of the slice: x: 2, y: 2, z: 4 (z_hi: 2, z_lo: 2; z = z_hi * 2 + z_lo), core: 2. Of those that a mesh axis runs over, the one named last changes fastest.
Arguments:
- tokens: bfloat16 [2048, 2048], P(('dp', 'expert')), may hold values from -6 to 6
- expert_ids: int32 [2048, 8], P(('dp', 'expert')), may hold values from 0 to 15, all different within a row; in each aligned block of 64 rows (0 to 63, 64 to 127, ...) at most 64 rows name the same one
- weights: bfloat16 [2, 16, 768, 2048], P(None, 'expert', 'tensor'), may hold values from -0.125 to 0.125
- first_moment: bfloat16 [2, 16, 768, 2048], P('dp', 'expert', 'tensor'), may hold values from -6 to 6
- second_moment: bfloat16 [2, 16, 768, 2048], P('dp', 'expert', 'tensor'), may hold values from 1 to 100
- hidden_grad: bfloat16 [2, 16, 768, 1024], P('dp', 'expert', 'tensor'), may hold values from -6 to 6
- swap_list: int32 [4, 2], replicated, may hold values from 0 to 15, as said below
Outputs:
- hidden: bfloat16 [2, 16, 768, 1024], P('dp', 'expert', 'tensor')
- token_grad: bfloat16 [2048, 2048], P(('dp', 'expert', 'tensor'))
- new_weights: bfloat16 [2, 16, 768, 2048], P('dp', 'expert', 'tensor')
- new_first: bfloat16 [2, 16, 768, 2048], P('dp', 'expert', 'tensor')
- new_second: bfloat16 [2, 16, 768, 2048], P('dp', 'expert', 'tensor')
Inputs may be any that keep to these rules, and one draw needn't show every extreme that they name: `expert_ids`: each row names 8 different experts. Within the rows of one quarter block of 64 rows no expert is named by more than 64 rows, a bound that some block reaches. `swap_list`: expert e is owned by index e // 2 of expert. The owners of the two experts of a row are 4 indices apart, and no owner appears in two rows.
All inputs are finite; a program needn't handle non-finite values.
Results may differ from a plain program's by a relative error of at most 0.0065.
Values may be sent and summed in bfloat16 or wider, within the bound.
No kernel may reach another device: no remote copies, remote signals or barrier semaphores. Data moves between devices by JAX's collectives and lax.ppermute only.
A program may use at most 192 MiB of HBM per device.

v0:
```python
import jax
import jax.numpy as jnp
from jax import lax
from jax.sharding import PartitionSpec as P

beta_one = 0.9
beta_two = 0.95
step_size = 0.01
adam_eps = 1e-08


def partner(value, axis, bit):
    return lax.ppermute(value, axis, [(i, i ^ 1 << bit) for i in range(lax.axis_size(axis))])


def slot_select(expert_ids, blocks, per_dev, owners, capacity):
    row_total = expert_ids.shape[0]
    top_count = expert_ids.shape[1]
    pair_total = row_total * top_count
    block_pairs = pair_total // blocks
    expert_total = per_dev * owners
    named_flat = expert_ids.reshape(blocks, block_pairs)
    one_hot = (
        named_flat[:, :, None] == jnp.arange(expert_total, dtype=jnp.int32)[None, None, :]
    ).astype(jnp.int32)
    slot_rank = (jnp.sum(jnp.cumsum(one_hot, axis=1) * one_hot, axis=2) - 1).reshape(pair_total)
    block_index = jnp.arange(pair_total, dtype=jnp.int32) // block_pairs
    expert_flat = named_flat.reshape(pair_total)
    slot_key = (
        (expert_flat % per_dev * owners + expert_flat // per_dev) * blocks + block_index
    ) * capacity + slot_rank
    key_total = expert_total * blocks * capacity
    by_key = (jnp.arange(key_total, dtype=jnp.int32)[:, None] == slot_key[None, :]).astype(
        jnp.bfloat16
    )
    pair_rows = jnp.arange(pair_total, dtype=jnp.int32) // top_count
    by_row = (pair_rows[:, None] == jnp.arange(row_total, dtype=jnp.int32)[None, :]).astype(
        jnp.bfloat16
    )
    return jnp.dot(by_key, by_row, preferred_element_type=jnp.float32).astype(jnp.bfloat16)


def migration_slot(swap_list, per_dev):
    own_index = lax.axis_index("expert")
    first_hit = swap_list[:, 0] // per_dev == own_index
    second_hit = swap_list[:, 1] // per_dev == own_index
    chosen = jnp.sum(
        jnp.where(first_hit, swap_list[:, 0] % per_dev, 0)
        + jnp.where(second_hit, swap_list[:, 1] % per_dev, 0)
    )
    return (chosen, jnp.any(first_hit | second_hit))


def pick_slot(state, chosen):
    return lax.dynamic_index_in_dim(state, chosen, 1, keepdims=False)


def place_slot(state, incoming, chosen, moving):
    target = (jnp.arange(state.shape[1], dtype=jnp.int32) == chosen) & moving
    return jnp.where(target[None, :, None, None], incoming[:, None], state)


def adam_step(weight_half, first_moment, second_moment, weight_grad):
    first_next = beta_one * first_moment.astype(jnp.float32) + (1.0 - beta_one) * weight_grad
    second_next = (
        beta_two * second_moment.astype(jnp.float32) + (1.0 - beta_two) * weight_grad * weight_grad
    )
    updated = weight_half.astype(jnp.float32) - step_size * first_next / (
        jnp.sqrt(second_next) + adam_eps
    )
    return (
        updated.astype(jnp.bfloat16),
        first_next.astype(jnp.bfloat16),
        second_next.astype(jnp.bfloat16),
    )


def shards(tokens, expert_ids, weights, first_moment, second_moment, hidden_grad, swap_list):
    owners = lax.axis_size("expert")
    tensor_count = lax.axis_size("tensor")
    replicas = lax.axis_size("dp")
    per_dev = weights.shape[1]
    model_width = tokens.shape[1]
    slots_total = hidden_grad.shape[3]
    capacity = slots_total // (owners * tensor_count)
    quarter_rows = tokens.shape[0] // tensor_count
    quarter_index = lax.axis_index("tensor")
    whole_select = slot_select(expert_ids, tensor_count, per_dev, owners, capacity)
    outgoing = jnp.dot(whole_select, tokens, preferred_element_type=jnp.float32).astype(
        jnp.bfloat16
    )
    outgoing = outgoing.reshape(per_dev, owners, tensor_count * capacity, model_width)
    arrived = lax.all_to_all(outgoing, "expert", split_axis=1, concat_axis=1, tiled=True)
    select_grid = whole_select.reshape(
        per_dev, owners, tensor_count, capacity, tensor_count, quarter_rows
    )
    select_grid = lax.dynamic_index_in_dim(select_grid, quarter_index, 2, keepdims=False)
    select_grid = lax.dynamic_index_in_dim(select_grid, quarter_index, 3, keepdims=False)
    own_select = select_grid.reshape(per_dev * owners * capacity, quarter_rows)
    routed = arrived.reshape(per_dev, slots_total, model_width)
    half_rows = 2 // replicas
    replica_index = lax.axis_index("dp")
    weight_half = lax.dynamic_slice_in_dim(weights, replica_index * half_rows, half_rows, 0)
    chosen, moving = migration_slot(swap_list, per_dev)
    top_bit = owners.bit_length() - 2
    projected = jnp.einsum("cefd,esd->ecfs", weights, routed, preferred_element_type=jnp.float32)
    gate_pre = projected[:, 0]
    up_pre = projected[:, 1]
    sigmoid_gate = jax.nn.sigmoid(gate_pre)
    hidden = (gate_pre * sigmoid_gate * up_pre).astype(jnp.bfloat16)
    grad_hidden = hidden_grad[0].astype(jnp.float32)
    grad_gate = grad_hidden * up_pre * sigmoid_gate * (1.0 + gate_pre * (1.0 - sigmoid_gate))
    grad_up = grad_hidden * gate_pre * sigmoid_gate
    grad_pre = jnp.stack([grad_gate, grad_up], axis=1).astype(jnp.bfloat16)
    slot_terms = jnp.einsum("ecfs,cefd->esd", grad_pre, weights, preferred_element_type=jnp.float32)
    slot_terms = slot_terms.reshape(per_dev, owners, tensor_count, capacity, model_width)
    summed = lax.psum_scatter(
        slot_terms.astype(jnp.bfloat16), "tensor", scatter_dimension=2, tiled=True
    )
    returning = summed.reshape(per_dev, owners, capacity, model_width)
    back_rows = lax.all_to_all(returning, "expert", split_axis=1, concat_axis=1, tiled=True)
    token_grad = jnp.dot(
        own_select.T,
        back_rows.reshape(per_dev * owners * capacity, model_width),
        preferred_element_type=jnp.float32,
    ).astype(jnp.bfloat16)

    def grad_rows(offset, number):
        part_grad = lax.dynamic_slice_in_dim(grad_pre, offset, number, 1)
        return jnp.einsum("esd,ecfs->cefd", routed, part_grad, preferred_element_type=jnp.float32)

    own_term = grad_rows(replica_index * half_rows, half_rows)
    other_term = grad_rows((1 - replica_index) * half_rows, half_rows)
    weight_grad = own_term + partner(other_term, "dp", 0)
    updated, first_next, second_next = adam_step(
        weight_half, first_moment, second_moment, weight_grad
    )
    arrived_states = partner(
        (pick_slot(updated, chosen), pick_slot(first_next, chosen), pick_slot(second_next, chosen)),
        "expert",
        top_bit,
    )
    new_weights = place_slot(updated, arrived_states[0], chosen, moving)
    new_first = place_slot(first_next, arrived_states[1], chosen, moving)
    new_second = place_slot(second_next, arrived_states[2], chosen, moving)
    return (hidden[None], token_grad, new_weights, new_first, new_second)


def solution(mesh):
    in_specs = (
        P(("dp", "expert"), None),
        P(("dp", "expert"), None),
        P(None, "expert", "tensor", None),
        P("dp", "expert", "tensor", None),
        P("dp", "expert", "tensor", None),
        P("dp", "expert", "tensor", None),
        P(),
    )
    out_specs = (
        P("dp", "expert", "tensor", None),
        P(("dp", "expert", "tensor"), None),
        P("dp", "expert", "tensor", None),
        P("dp", "expert", "tensor", None),
        P("dp", "expert", "tensor", None),
    )
    return jax.shard_map(shards, mesh=mesh, in_specs=in_specs, out_specs=out_specs, check_vma=False)
```

profile of v0, /device:TPU:27, one launch (start us, length us, event | category | flops | bytes accessed | tf_op | source)
XLA Modules:
  0.0 668.8 jit_solution(12819132871745916266)
XLA Ops:
  8.3 2.3 reduce-window.6
  11.1 1.6 fusion.20
  12.8 5.6 convolution_convert_fusion
  18.3 8.3 %copy.45 = bf16[2,8,128,2048]{3,2,0,1:T(8,128)(2,1)} copy(bf16[2,8,128,2048]{3,2,1,0:T(8,128)(2,1)} %bitcast.124) | data formatting | bytes 16777216 | tf_op jit(solution)/shard_map/reshape | solution.py:92
  26.6 5.7 all-to-all-start
  32.4 1.9 copy.49
  34.2 90.7 %all-to-all-done = bf16[2,8,128,2048]{3,2,0,1:T(8,128)(2,1)} async-done(((bf16[2,8,128,2048]{3,2,0,1:T(8,128)(2,1)}), bf16[2,8,128,2048]{3,2,0,1:T(8,128)(2,1)}, u32[]{:S(2)}, u32[]{:S(2)}) %all-to-all-start) | async-done | bytes 8388640 | tf_op jit(solution)/shard_map/all_to_all | solution.py:93
  124.9 8.4 %copy.46 = bf16[2,8,128,2048]{3,2,1,0:T(8,128)(2,1)} copy(bf16[2,8,128,2048]{3,2,0,1:T(8,128)(2,1)} %all-to-all-done) | data formatting | bytes 16777216 | tf_op jit(solution)/shard_map/all_to_all | solution.py:93
  133.3 10.2 %fusion.17 = f32[2,2,384,1024]{2,3,1,0:T(8,128)S(1)} fusion(bf16[2,1024,2048,1]{2,1,3,0:T(8,128)(2,1)} %bitcast.126, bf16[2,2,384,2048]{3,2,1,0:T(8,128)(2,1)} %param.9), kind=kOutput, calls=%fused_computation.40 | convolution fusion | flops 6442450944 | bytes 20971520 | tf_op jit(solution)/shard_map/cefd,esd->ecfs/dot_general | solution.py:106
  143.6 1.6 fusion.10
  146.3 8.9 %bitcast_convert_fusion = bf16[2,1024,2048]{2,1,0:T(8,128)(2,1)} fusion(bf16[2,2,384,2048]{3,2,1,0:T(8,128)(2,1)S(1)} %bitcast.133, bf16[2,1,384,1024]{2,3,1,0:T(8,128)(2,1)S(1)} %get-tuple-element.32, bf16[2,1,384,1024]{2,3,1,0:T(8,128)(2,1)S(1)} %get-tuple-element.31), kind=kOutput, calls=%fused_computation | convolution fusion | flops 6448218112 | bytes 17825792 | tf_op jit(solution)/shard_map/ecfs,cefd->esd/dot_general | solution.py:115
  156.6 9.6 %convolution_bitcast_fusion = f32[1,2,384,2048]{3,2,1,0:T(8,128)} fusion(bf16[2,1024,2048]{2,1,0:T(8,128)(2,1)} %bitcast.127, s32[]{:T(128)S(6)} %select_n.103, bf16[2,1,384,1024]{2,3,1,0:T(8,128)(2,1)S(1)} %copy-done.7, bf16[2,1,384,1024]{2,3,1,0:T(8,128)(2,1)} %copy-done.8), kind=kOutput, calls=%fused_computation.21 | convolution fusion | flops 3222011904 | bytes 17825796 | tf_op jit(solution)/shard_map/esd,ecfs->cefd/dot_general | solution.py:130
  170.0 321.0 %all-reduce.3.cloned.1.call-done = bf16[2,8,2,64,2048]{4,3,2,1,0:T(8,128)(2,1)} async-done(((bf16[2,8,2,64,2048]{4,3,2,1,0:T(8,128)(2,1)}), bf16[2,8,2,64,2048]{4,3,2,1,0:T(8,128)(2,1)}) %all-reduce.3.cloned.1.call-update) | async-done | bytes 8388624
  491.0 3.1 dynamic-slice_bitcast_fusion
  494.1 2.2 copy.51
  496.4 4.7 all-to-all-start.1
  501.1 14.5 %fusion.7 = (bf16[1,2,384,2048]{3,2,1,0:T(8,128)(2,1)S(1)}, bf16[1,2,384,2048]{3,2,1,0:T(8,128)(2,1)S(1)}, bf16[1,2,384,2048]{3,2,1,0:T(8,128)(2,1)}) fusion(bf16[1,2,384,2048]{3,2,1,0:T(8,128)(2,1)} %param.11, bf16[1,2,384,2048]{3,2,1,0:T(8,128)(2,1)} %param.10, bf16[2,2,384,2048]{3,2,1,0:T(8,128)(2,1)} %param.9, s32[]{:T(128)S(6)} %select_n.102, ...), kind=kOutput, calls=%fused_computation.23 | convolution fusion | flops 3250323456 | bytes 36701184 | tf_op jit(solution)/shard_map/esd,ecfs->cefd/dot_general | solution.py:130
  525.6 3.7 fusion.13
  529.3 1.6 copy.55
  530.9 50.3 %collective-permute-done.2 = bf16[1,384,2048]{2,1,0:T(8,128)(2,1)} collective-permute-done((bf16[1,384,2048]{2,1,0:T(8,128)(2,1)}, bf16[1,384,2048]{2,1,0:T(8,128)(2,1)}, u32[]{:S(2)}, u32[]{:S(2)}) %collective-permute-start.2) | collective-permute-done | bytes 1572896 | tf_op jit(solution)/shard_map/ppermute | solution.py:13
  581.3 33.7 %collective-permute-done.1 = bf16[1,384,2048]{2,1,0:T(8,128)(2,1)} collective-permute-done((bf16[1,384,2048]{2,1,0:T(8,128)(2,1)}, bf16[1,384,2048]{2,1,0:T(8,128)(2,1)}, u32[]{:S(2)}, u32[]{:S(2)}) %collective-permute-start.1) | collective-permute-done | bytes 1572896 | tf_op jit(solution)/shard_map/ppermute | solution.py:13
  615.0 33.7 %collective-permute-done.3 = bf16[1,384,2048]{2,1,0:T(8,128)(2,1)} collective-permute-done((bf16[1,384,2048]{2,1,0:T(8,128)(2,1)}, bf16[1,384,2048]{2,1,0:T(8,128)(2,1)}, u32[]{:S(2)}, u32[]{:S(2)}) %collective-permute-start.3) | collective-permute-done | bytes 1572896 | tf_op jit(solution)/shard_map/ppermute | solution.py:13
  648.7 9.1 %broadcast_select_fusion = (bf16[1,2,384,2048]{3,2,1,0:T(8,128)(2,1)}, bf16[1,2,384,2048]{3,2,1,0:T(8,128)(2,1)}, bf16[1,2,384,2048]{3,2,1,0:T(8,128)(2,1)}) fusion(bf16[1,2,384,2048]{3,2,1,0:T(8,128)(2,1)} %copy-done.3, pred[2]{0:T(512)(128)(4,1)S(1)} %compare_and_fusion, bf16[384,2048]{1,0:T(8,128)(2,1)} %bitcast.26, ...), kind=kLoop, calls=%fused_computation.37 | loop fusion | flops 4718592 | bytes 23592962 | tf_op jit(solution)/shard_map/jit(_where)/select_n | solution.py:60
  657.8 2.6 copy.52
  (58 shorter events, 17.4 us)
Async XLA Ops:
  7.2 5.6 copy-start
  26.6 98.3 %all-to-all-start = ((bf16[2,8,128,2048]{3,2,0,1:T(8,128)(2,1)}), bf16[2,8,128,2048]{3,2,0,1:T(8,128)(2,1)}, u32[]{:S(2)}, u32[]{:S(2)}) async-start(bf16[2,8,128,2048]{3,2,0,1:T(8,128)(2,1)} %copy.45), calls=%async_computation | async-start | bytes 16777216 | tf_op jit(solution)/shard_map/all_to_all | solution.py:93
  32.3 458.6 %all-reduce.3.cloned.1.call-start = ((), (), s32[]{:S(2)}) async-start(), calls=%async_computation.2 | async-start | bytes 16777216
  124.9 21.4 %slice-start = ((s8[6291456]{0:T(1024)(128)(4,1)}), s8[2097152]{0:T(1024)(128)(4,1)S(1)}, s32[]{:S(2)}) async-start(s8[6291456]{0:T(1024)(128)(4,1)} %bitcast.132), calls=%async_computation.3 | async-start | bytes 4194304
  133.3 12.9 %slice-start.1 = ((s8[6291456]{0:T(1024)(128)(4,1)}), s8[4194304]{0:T(1024)(128)(4,1)S(1)}, s32[]{:S(2)}) async-start(s8[6291456]{0:T(1024)(128)(4,1)} %bitcast.132), calls=%async_computation.4 | async-start | bytes 8388608
  143.6 2.7 copy-start.2
  146.3 8.9 %copy-start.6 = (bf16[2,1,384,1024]{2,3,1,0:T(8,128)(2,1)}, bf16[2,1,384,1024]{2,3,1,0:T(8,128)(2,1)S(1)}, u32[]{:S(2)}) copy-start(bf16[2,1,384,1024]{2,3,1,0:T(8,128)(2,1)S(1)} %get-tuple-element.31) | copy-start | bytes 4718596
  146.3 8.9 %copy-start.8 = (bf16[2,1,384,1024]{2,3,1,0:T(8,128)(2,1)}, bf16[2,1,384,1024]{2,3,1,0:T(8,128)(2,1)S(1)}, u32[]{:S(2)}) copy-start(bf16[2,1,384,1024]{2,3,1,0:T(8,128)(2,1)S(1)} %get-tuple-element.32) | copy-start | bytes 4718596
  155.2 1.4 copy-start.7
  156.6 10.1 %copy-start.9 = (s32[4,2]{0,1:T(2,128)S(1)}, s32[4,2]{0,1:T(2,128)}, u32[]{:S(2)}) copy-start(s32[4,2]{0,1:T(2,128)} %param.13) | copy-start | bytes 100
  156.6 12.1 %copy-start.10 = (u32[32]{0:T(128)S(1)}, u32[32]{0:T(128)}, u32[]{:S(2)}) copy-start(u32[32]{0:T(128)} %constant.173) | copy-start | bytes 388
  166.2 334.9 %collective-permute-start = (f32[1,2,384,2048]{3,2,1,0:T(8,128)}, f32[1,2,384,2048]{3,2,1,0:T(8,128)}, u32[]{:S(2)}, u32[]{:S(2)}) collective-permute-start(f32[1,2,384,2048]{3,2,1,0:T(8,128)} %convolution_bitcast_fusion), channel_id=1, source_target_pairs={{0,16},{16,0},{1,17},{17,1},{2,18},{18,2},{3,19},{19,3},{4,20},{20... | collective-permute-start | bytes 18874376 | tf_op jit(solution)/shard_map/ppermute | solution.py:13
  496.4 161.5 %all-to-all-start.1 = ((bf16[2,8,64,2048]{3,2,0,1:T(8,128)(2,1)}), bf16[2,8,64,2048]{3,2,0,1:T(8,128)(2,1)}, u32[]{:S(2)}, u32[]{:S(2)}) async-start(bf16[2,8,64,2048]{3,2,0,1:T(8,128)(2,1)} %copy.51), calls=%async_computation.1 | async-start | bytes 8388608 | tf_op jit(solution)/shard_map/all_to_all | solution.py:121
  515.6 3.1 copy-start.3
  515.6 4.2 copy-start.4
  515.6 4.2 copy-start.5
  521.0 60.3 %collective-permute-start.2 = (bf16[1,384,2048]{2,1,0:T(8,128)(2,1)}, bf16[1,384,2048]{2,1,0:T(8,128)(2,1)}, u32[]{:S(2)}, u32[]{:S(2)}) collective-permute-start(bf16[1,384,2048]{2,1,0:T(8,128)(2,1)} %dynamic-slice_bitcast_fusion.2), channel_id=1, source_target_pairs={{0,8},{2,10},{4,12},{6,14},{8,0},{10,2},{12,4},{14,6},{1,9},{3,11}... | collective-permute-start | bytes 4718600 | tf_op jit(solution)/shard_map/ppermute | solution.py:13
  521.1 93.9 %collective-permute-start.1 = (bf16[1,384,2048]{2,1,0:T(8,128)(2,1)}, bf16[1,384,2048]{2,1,0:T(8,128)(2,1)}, u32[]{:S(2)}, u32[]{:S(2)}) collective-permute-start(bf16[1,384,2048]{2,1,0:T(8,128)(2,1)} %dynamic-slice_bitcast_fusion.3), channel_id=1, source_target_pairs={{0,8},{2,10},{4,12},{6,14},{8,0},{10,2},{12,4},{14,6},{1,9},{3,11}... | collective-permute-start | bytes 4718600 | tf_op jit(solution)/shard_map/ppermute | solution.py:13
  522.5 126.2 %collective-permute-start.3 = (bf16[1,384,2048]{2,1,0:T(8,128)(2,1)}, bf16[1,384,2048]{2,1,0:T(8,128)(2,1)}, u32[]{:S(2)}, u32[]{:S(2)}) collective-permute-start(bf16[1,384,2048]{2,1,0:T(8,128)(2,1)} %dynamic-slice_bitcast_fusion.1), channel_id=1, source_target_pairs={{0,8},{2,10},{4,12},{6,14},{8,0},{10,2},{12,4},{14,6},{1,9},{3,11}... | collective-permute-start | bytes 4718600 | tf_op jit(solution)/shard_map/ppermute | solution.py:13
  657.8 4.2 copy-start.1
Sparse Core Ops, SparseCore 0:
  155.4 335.5 all-reduce.2
where the time goes:
time: 669 us
  waiting for transfers between devices  530 us (79%)
  matrix products  52 us (8%)
  local copies, waits for them, and re-layouts  39.1 us (6%)
  other arithmetic  19.5 us (3%)
  between operations  16.2 us (2%)
  starting transfers between devices  12.6 us (2%)
    unnamed x2, waiting for transfers between devices  321 us
    ppermute x4, waiting for transfers between devices, partner(): lax.ppermute(value, axis, [(i, i ^ 1 << bit) for i in range(lax.axis_size...  118 us
    all_to_all x1, waiting for transfers between devices, shards(): lax.all_to_all(outgoing, 'expert', split_axis=1, concat_axis=1, tiled=True)  90.7 us
    dot_general x2, matrix products, grad_rows(): jnp.einsum('esd,ecfs->cefd', routed, part_grad, preferred_element_type=jn...  24.1 us
  transfers between devices with their start and end apart: 7, of which 5 were waited for; matrix products, arithmetic and copies ran while one was open for 8% of the time, Pallas kernels for 0%

commit v1 on v0

--- a/solution.py
+++ b/solution.py
@@ -7,6 +7,29 @@
 beta_two = 0.95
 step_size = 0.01
 adam_eps = 1e-08
+
+
+def split_up(shard, dim, peers):
+    lengths = shard.shape
+    blocks = shard.reshape(*lengths[:dim], peers, lengths[dim] // peers, *lengths[dim + 1 :])
+    return jnp.moveaxis(blocks, dim, 0)
+
+
+def joined_along(blocks, dim):
+    lengths = list(blocks.shape[1:])
+    lengths[dim] *= blocks.shape[0]
+    return jnp.moveaxis(blocks, 0, dim).reshape(lengths)
+
+
+def exchange_in_pairs(x, axis, split_dim, concat_dim):
+    devices, index = (lax.axis_size(axis), lax.axis_index(axis))
+    blocks = split_up(x, split_dim, devices)
+    outs = [blocks[index]]
+    for step in range(1, devices):
+        sent = blocks[index ^ step]
+        outs.append(lax.ppermute(sent, axis, [(i, i ^ step) for i in range(devices)]))
+    blocks = jnp.stack(outs)[index ^ jnp.arange(devices)]
+    return joined_along(blocks, concat_dim)
 
 
 def partner(value, axis, bit):
@@ -90,7 +113,7 @@
         jnp.bfloat16
     )
     outgoing = outgoing.reshape(per_dev, owners, tensor_count * capacity, model_width)
-    arrived = lax.all_to_all(outgoing, "expert", split_axis=1, concat_axis=1, tiled=True)
+    arrived = exchange_in_pairs(outgoing, "expert", 1, 1)
     select_grid = whole_select.reshape(
         per_dev, owners, tensor_count, capacity, tensor_count, quarter_rows
     )

time: 669 us -> 683 us (1.021)
  local copies, waits for them, and re-layouts: 39.1 us -> 60.5 us
  waiting for transfers between devices: 530 us -> 519 us
    all_to_all x1 -> x0, waiting for transfers between devices: 90.7 us -> none  [shards(): lax.all_to_all(outgoing, 'expert', split_axis=1, concat_axis=1, tiled=True)]
    ppermute x0 -> x7, waiting for transfers between devices: none -> 80.7 us  [exchange_in_pairs(): lax.ppermute(sent, axis, [(i, i ^ step) for i in range(devices)])]
    unnamed x32 -> x41, local copies, waits for them, and re-layouts: 8.94 us -> 25 us
    ppermute x0 -> x7, starting transfers between devices: none -> 8.83 us  [exchange_in_pairs(): lax.ppermute(sent, axis, [(i, i ^ step) for i in range(devices)])]
    transpose x0 -> x1, local copies, waits for them, and re-layouts: none -> 8.42 us  [joined_along(): return jnp.moveaxis(blocks, 0, dim).reshape(lengths)]
    all_to_all x1 -> x0, local copies, waits for them, and re-layouts: 8.42 us -> none  [shards(): lax.all_to_all(outgoing, 'expert', split_axis=1, concat_axis=1, tiled=True)]
    reshape x1 -> x0, local copies, waits for them, and re-layouts: 8.27 us -> none  [shards(): outgoing.reshape(per_dev, owners, tensor_count * capacity, model_width)]
    gather x0 -> x1, local copies, waits for them, and re-layouts: none -> 8.06 us  [exchange_in_pairs(): blocks = jnp.stack(outs)[index ^ jnp.arange(devices)]]
  transfers between devices with their start and end apart: 7 -> 13, of which waited for: 5 -> 7; matrix products, arithmetic and copies ran while one was open for 8% -> 10% of each run, Pallas kernels for 0% -> 0%
where the time goes in v1:
time: 683 us; the launch traced here: 682 us
  waiting for transfers between devices  519 us (76%)
  local copies, waits for them, and re-layouts  60.5 us (9%)
  matrix products  48.9 us (7%)
  other arithmetic  19.5 us (3%)
  starting transfers between devices  17.6 us (3%)
  between operations  16.3 us (2%)
    unnamed x2, waiting for transfers between devices  321 us
    ppermute x4, waiting for transfers between devices, partner(): lax.ppermute(value, axis, [(i, i ^ 1 << bit) for i in range(lax.axis_size...  118 us
    ppermute x7, waiting for transfers between devices, exchange_in_pairs(): lax.ppermute(sent, axis, [(i, i ^ step) for i in range(devices)])  80.7 us
    unnamed x41, local copies, waits for them, and re-layouts  25 us
    dot_general x2, matrix products, grad_rows(): jnp.einsum('esd,ecfs->cefd', routed, part_grad, preferred_element_type=jn...  24 us
  transfers between devices with their start and end apart: 13, of which 7 were waited for; matrix products, arithmetic and copies ran while one was open for 10% of the time, Pallas kernels for 0%

profile of v1, /device:TPU:27, one launch (start us, length us, event | category | flops | bytes accessed | tf_op | source)
XLA Modules:
  0.0 682.1 jit_solution(7177296306694222611)
XLA Ops:
  15.2 3.1 dynamic-slice_bitcast_fusion.4
  18.4 2.3 copy-done.2
  21.6 2.3 collective-permute-start.6
  25.8 2.4 bitcast_dynamic-update-slice_fusion.7
  33.7 12.7 %collective-permute-done.1 = bf16[2,1,128,2048]{3,2,0,1:T(8,128)(2,1)} collective-permute-done((bf16[2,1,128,2048]{3,2,0,1:T(8,128)(2,1)}, bf16[2,1,128,2048]{3,2,0,1:T(8,128)(2,1)}, u32[]{:S(2)}, u32[]{:S(2)}) %collective-permute-start.1) | collective-permute-done | bytes 1048608 | tf_op jit(solution)/shard_map/ppermute | solution.py:30
  46.4 2.5 collective-permute-start.4
  51.2 63.1 %collective-permute-done.2 = bf16[2,1,128,2048]{3,2,0,1:T(8,128)(2,1)} collective-permute-done((bf16[2,1,128,2048]{3,2,0,1:T(8,128)(2,1)}, bf16[2,1,128,2048]{3,2,0,1:T(8,128)(2,1)}, u32[]{:S(2)}, u32[]{:S(2)}) %collective-permute-start.2) | collective-permute-done | bytes 1048608 | tf_op jit(solution)/shard_map/ppermute | solution.py:30
  114.2 2.3 bitcast_dynamic-update-slice_fusion.4
  117.7 5.0 collective-permute-done.4
  128.3 8.1 %gather_fusion = bf16[8,2,128,2048]{3,2,1,0:T(8,128)(2,1)} fusion(bf16[8,2,128,2048]{3,2,1,0:T(8,128)(2,1)} %bitcast.164, s32[1024]{0:T(1024)S(1)} %pad_clamp_fusion), kind=kCustom, calls=%fused_computation | custom fusion | bytes 16777248 | tf_op jit(solution)/shard_map/gather | solution.py:31
  136.3 8.4 %copy.56 = bf16[2,8,1,128,2048]{4,3,1,0,2:T(8,128)(2,1)} copy(bf16[2,8,1,128,2048]{4,3,0,1,2:T(8,128)(2,1)} %bitcast.162) | data formatting | bytes 16777216 | tf_op jit(solution)/shard_map/transpose | solution.py:21
  144.8 10.2 %fusion.17 = f32[2,2,384,1024]{2,3,1,0:T(8,128)S(1)} fusion(bf16[2,1024,2048,1]{2,1,3,0:T(8,128)(2,1)} %bitcast.165, bf16[2,2,384,2048]{3,2,1,0:T(8,128)(2,1)} %param.9), kind=kOutput, calls=%fused_computation.41 | convolution fusion | flops 6442450944 | bytes 20971520 | tf_op jit(solution)/shard_map/cefd,esd->ecfs/dot_general | solution.py:129
  157.7 9.1 %bitcast_convert_fusion = bf16[2,1024,2048]{2,1,0:T(8,128)(2,1)} fusion(bf16[2,2,384,2048]{3,2,1,0:T(8,128)(2,1)S(1)} %bitcast.172, bf16[2,1,384,1024]{2,3,1,0:T(8,128)(2,1)S(1)} %get-tuple-element.44, bf16[2,1,384,1024]{2,3,1,0:T(8,128)(2,1)S(1)} %get-tuple-element.43), kind=kOutput, calls=%fused_computation.1 | convolution fusion | flops 6448218112 | bytes 17825792 | tf_op jit(solution)/shard_map/ecfs,cefd->esd/dot_general | solution.py:138
  168.3 9.6 %convolution_bitcast_fusion = f32[1,2,384,2048]{3,2,1,0:T(8,128)} fusion(bf16[2,1024,2048]{2,1,0:T(8,128)(2,1)} %bitcast.166, s32[]{:T(128)S(6)} %select_n.146, bf16[2,1,384,1024]{2,3,1,0:T(8,128)(2,1)S(1)} %copy-done.8, bf16[2,1,384,1024]{2,3,1,0:T(8,128)(2,1)} %copy-done.9), kind=kOutput, calls=%fused_computation.22 | convolution fusion | flops 3222011904 | bytes 17825796 | tf_op jit(solution)/shard_map/esd,ecfs->cefd/dot_general | solution.py:153
  181.6 320.7 %all-reduce.3.cloned.1.call-done = bf16[2,8,2,64,2048]{4,3,2,1,0:T(8,128)(2,1)} async-done(((bf16[2,8,2,64,2048]{4,3,2,1,0:T(8,128)(2,1)}), bf16[2,8,2,64,2048]{4,3,2,1,0:T(8,128)(2,1)}) %all-reduce.3.cloned.1.call-update) | async-done | bytes 8388624
  502.3 3.1 dynamic-slice_bitcast_fusion
  507.7 5.5 all-to-all-start
  513.2 14.4 %fusion.7 = (bf16[1,2,384,2048]{3,2,1,0:T(8,128)(2,1)S(1)}, bf16[1,2,384,2048]{3,2,1,0:T(8,128)(2,1)S(1)}, bf16[1,2,384,2048]{3,2,1,0:T(8,128)(2,1)}) fusion(bf16[1,2,384,2048]{3,2,1,0:T(8,128)(2,1)} %param.11, bf16[1,2,384,2048]{3,2,1,0:T(8,128)(2,1)} %param.10, bf16[2,2,384,2048]{3,2,1,0:T(8,128)(2,1)} %param.9, s32[]{:T(128)S(6)} %select_n.145, ...), kind=kOutput, calls=%fused_computation.24 | convolution fusion | flops 3250323456 | bytes 36701184 | tf_op jit(solution)/shard_map/esd,ecfs->cefd/dot_general | solution.py:153
  538.7 3.7 fusion.13
  544.1 50.4 %collective-permute-done.9 = bf16[1,384,2048]{2,1,0:T(8,128)(2,1)} collective-permute-done((bf16[1,384,2048]{2,1,0:T(8,128)(2,1)}, bf16[1,384,2048]{2,1,0:T(8,128)(2,1)}, u32[]{:S(2)}, u32[]{:S(2)}) %collective-permute-start.9) | collective-permute-done | bytes 1572896 | tf_op jit(solution)/shard_map/ppermute | solution.py:36
  594.5 33.7 %collective-permute-done.8 = bf16[1,384,2048]{2,1,0:T(8,128)(2,1)} collective-permute-done((bf16[1,384,2048]{2,1,0:T(8,128)(2,1)}, bf16[1,384,2048]{2,1,0:T(8,128)(2,1)}, u32[]{:S(2)}, u32[]{:S(2)}) %collective-permute-start.8) | collective-permute-done | bytes 1572896 | tf_op jit(solution)/shard_map/ppermute | solution.py:36
  628.2 33.7 %collective-permute-done.10 = bf16[1,384,2048]{2,1,0:T(8,128)(2,1)} collective-permute-done((bf16[1,384,2048]{2,1,0:T(8,128)(2,1)}, bf16[1,384,2048]{2,1,0:T(8,128)(2,1)}, u32[]{:S(2)}, u32[]{:S(2)}) %collective-permute-start.10) | collective-permute-done | bytes 1572896 | tf_op jit(solution)/shard_map/ppermute | solution.py:36
  661.9 9.1 %broadcast_select_fusion = (bf16[1,2,384,2048]{3,2,1,0:T(8,128)(2,1)}, bf16[1,2,384,2048]{3,2,1,0:T(8,128)(2,1)}, bf16[1,2,384,2048]{3,2,1,0:T(8,128)(2,1)}) fusion(bf16[1,2,384,2048]{3,2,1,0:T(8,128)(2,1)} %copy-done.4, pred[2]{0:T(512)(128)(4,1)S(1)} %compare_and_fusion, bf16[384,2048]{1,0:T(8,128)(2,1)} %bitcast.45, ...), kind=kLoop, calls=%fused_computation.38 | loop fusion | flops 4718592 | bytes 23592962 | tf_op jit(solution)/shard_map/jit(_where)/select_n | solution.py:83
  671.1 2.6 copy.62
  (83 shorter events, 47.7 us)
Async XLA Ops:
  7.2 5.7 copy-start
  7.2 495.1 %all-reduce.3.cloned.1.call-start = ((), (), s32[]{:S(2)}) async-start(), calls=%async_computation.1 | async-start | bytes 16777216
  15.2 5.5 copy-start.2
  20.7 9.3 %collective-permute-start = (bf16[2,1,128,2048]{3,2,0,1:T(8,128)(2,1)}, bf16[2,1,128,2048]{3,2,0,1:T(8,128)(2,1)}, u32[]{:S(2)}, u32[]{:S(2)}) collective-permute-start(bf16[2,1,128,2048]{3,2,0,1:T(8,128)(2,1)} %get-tuple-element.42), channel_id=1, source_target_pairs={{0,2},{2,0},{4,6},{6,4},{8,10},{10,8},{12,14},{14,12},{1,3},{3,1},... | collective-permute-start | bytes 3145736 | tf_op jit(solution)/shard_map/ppermute | solution.py:30
  21.4 25.0 %collective-permute-start.1 = (bf16[2,1,128,2048]{3,2,0,1:T(8,128)(2,1)}, bf16[2,1,128,2048]{3,2,0,1:T(8,128)(2,1)}, u32[]{:S(2)}, u32[]{:S(2)}) collective-permute-start(bf16[2,1,128,2048]{3,2,0,1:T(8,128)(2,1)} %get-tuple-element.41), channel_id=1, source_target_pairs={{0,4},{2,6},{4,0},{6,2},{8,12},{10,14},{12,8},{14,10},{1,5},{3,7},... | collective-permute-start | bytes 3145736 | tf_op jit(solution)/shard_map/ppermute | solution.py:30
  21.6 104.3 %collective-permute-start.6 = (bf16[2,1,128,2048]{3,2,0,1:T(8,128)(2,1)}, bf16[2,1,128,2048]{3,2,0,1:T(8,128)(2,1)}, u32[]{:S(2)}, u32[]{:S(2)}) collective-permute-start(bf16[2,1,128,2048]{3,2,0,1:T(8,128)(2,1)} %get-tuple-element.36), channel_id=1, source_target_pairs={{0,14},{2,12},{4,10},{6,8},{8,6},{10,4},{12,2},{14,0},{1,15},{3,13... | collective-permute-start | bytes 3145736 | tf_op jit(solution)/shard_map/ppermute | solution.py:30
  24.0 99.7 %collective-permute-start.5 = (bf16[2,1,128,2048]{3,2,0,1:T(8,128)(2,1)}, bf16[2,1,128,2048]{3,2,0,1:T(8,128)(2,1)}, u32[]{:S(2)}, u32[]{:S(2)}) collective-permute-start(bf16[2,1,128,2048]{3,2,0,1:T(8,128)(2,1)} %get-tuple-element.37), channel_id=1, source_target_pairs={{0,12},{2,14},{4,8},{6,10},{8,4},{10,6},{12,0},{14,2},{1,13},{3,15... | collective-permute-start | bytes 3145736 | tf_op jit(solution)/shard_map/ppermute | solution.py:30
  24.1 90.1 %collective-permute-start.2 = (bf16[2,1,128,2048]{3,2,0,1:T(8,128)(2,1)}, bf16[2,1,128,2048]{3,2,0,1:T(8,128)(2,1)}, u32[]{:S(2)}, u32[]{:S(2)}) collective-permute-start(bf16[2,1,128,2048]{3,2,0,1:T(8,128)(2,1)} %get-tuple-element.40), channel_id=1, source_target_pairs={{0,6},{2,4},{4,2},{6,0},{8,14},{10,12},{12,10},{14,8},{1,7},{3,5},... | collective-permute-start | bytes 3145736 | tf_op jit(solution)/shard_map/ppermute | solution.py:30
  30.0 86.5 %collective-permute-start.3 = (bf16[2,1,128,2048]{3,2,0,1:T(8,128)(2,1)}, bf16[2,1,128,2048]{3,2,0,1:T(8,128)(2,1)S(1)}, u32[]{:S(2)}, u32[]{:S(2)}) collective-permute-start(bf16[2,1,128,2048]{3,2,0,1:T(8,128)(2,1)} %get-tuple-element.39), channel_id=1, source_target_pairs={{0,8},{2,10},{4,12},{6,14},{8,0},{10,2},{12,4},{14,6},{1,9},{3,11}... | collective-permute-start | bytes 3145736 | tf_op jit(solution)/shard_map/ppermute | solution.py:30
  46.4 76.2 %collective-permute-start.4 = (bf16[2,1,128,2048]{3,2,0,1:T(8,128)(2,1)}, bf16[2,1,128,2048]{3,2,0,1:T(8,128)(2,1)S(1)}, u32[]{:S(2)}, u32[]{:S(2)}) collective-permute-start(bf16[2,1,128,2048]{3,2,0,1:T(8,128)(2,1)} %get-tuple-element.38), channel_id=1, source_target_pairs={{0,10},{2,8},{4,14},{6,12},{8,2},{10,0},{12,6},{14,4},{1,11},{3,9}... | collective-permute-start | bytes 3145736 | tf_op jit(solution)/shard_map/ppermute | solution.py:30
  136.3 21.4 %slice-start = ((s8[6291456]{0:T(1024)(128)(4,1)}), s8[2097152]{0:T(1024)(128)(4,1)S(1)}, s32[]{:S(2)}) async-start(s8[6291456]{0:T(1024)(128)(4,1)} %bitcast.171), calls=%async_computation.2 | async-start | bytes 4194304
  144.8 12.9 %slice-start.1 = ((s8[6291456]{0:T(1024)(128)(4,1)}), s8[4194304]{0:T(1024)(128)(4,1)S(1)}, s32[]{:S(2)}) async-start(s8[6291456]{0:T(1024)(128)(4,1)} %bitcast.171), calls=%async_computation.3 | async-start | bytes 8388608
  157.7 9.2 %copy-start.7 = (bf16[2,1,384,1024]{2,3,1,0:T(8,128)(2,1)}, bf16[2,1,384,1024]{2,3,1,0:T(8,128)(2,1)S(1)}, u32[]{:S(2)}) copy-start(bf16[2,1,384,1024]{2,3,1,0:T(8,128)(2,1)S(1)} %get-tuple-element.43) | copy-start | bytes 4718596
  157.7 9.2 %copy-start.9 = (bf16[2,1,384,1024]{2,3,1,0:T(8,128)(2,1)}, bf16[2,1,384,1024]{2,3,1,0:T(8,128)(2,1)S(1)}, u32[]{:S(2)}) copy-start(bf16[2,1,384,1024]{2,3,1,0:T(8,128)(2,1)S(1)} %get-tuple-element.44) | copy-start | bytes 4718596
  168.3 10.2 %copy-start.10 = (s32[4,2]{0,1:T(2,128)S(1)}, s32[4,2]{0,1:T(2,128)}, u32[]{:S(2)}) copy-start(s32[4,2]{0,1:T(2,128)} %param.13) | copy-start | bytes 100
  168.3 12.1 %copy-start.11 = (u32[32]{0:T(128)S(1)}, u32[32]{0:T(128)}, u32[]{:S(2)}) copy-start(u32[32]{0:T(128)} %constant.183) | copy-start | bytes 388
  177.9 335.3 %collective-permute-start.7 = (f32[1,2,384,2048]{3,2,1,0:T(8,128)}, f32[1,2,384,2048]{3,2,1,0:T(8,128)}, u32[]{:S(2)}, u32[]{:S(2)}) collective-permute-start(f32[1,2,384,2048]{3,2,1,0:T(8,128)} %convolution_bitcast_fusion), channel_id=1, source_target_pairs={{0,16},{16,0},{1,17},{17,1},{2,18},{18,2},{3,19},{19,3},{4,20},{20... | collective-permute-start | bytes 18874376 | tf_op jit(solution)/shard_map/ppermute | solution.py:36
  507.7 163.4 %all-to-all-start = ((bf16[2,8,64,2048]{3,2,0,1:T(8,128)(2,1)}), bf16[2,8,64,2048]{3,2,0,1:T(8,128)(2,1)}, u32[]{:S(2)}, u32[]{:S(2)}) async-start(bf16[2,8,64,2048]{3,2,0,1:T(8,128)(2,1)} %copy.61), calls=%async_computation | async-start | bytes 8388608 | tf_op jit(solution)/shard_map/all_to_all | solution.py:144
  527.6 4.2 copy-start.5
  527.6 4.2 copy-start.6
  533.0 61.5 %collective-permute-start.9 = (bf16[1,384,2048]{2,1,0:T(8,128)(2,1)}, bf16[1,384,2048]{2,1,0:T(8,128)(2,1)}, u32[]{:S(2)}, u32[]{:S(2)}) collective-permute-start(bf16[1,384,2048]{2,1,0:T(8,128)(2,1)} %dynamic-slice_bitcast_fusion.2), channel_id=1, source_target_pairs={{0,8},{2,10},{4,12},{6,14},{8,0},{10,2},{12,4},{14,6},{1,9},{3,11}... | collective-permute-start | bytes 4718600 | tf_op jit(solution)/shard_map/ppermute | solution.py:36
  534.3 94.0 %collective-permute-start.8 = (bf16[1,384,2048]{2,1,0:T(8,128)(2,1)}, bf16[1,384,2048]{2,1,0:T(8,128)(2,1)}, u32[]{:S(2)}, u32[]{:S(2)}) collective-permute-start(bf16[1,384,2048]{2,1,0:T(8,128)(2,1)} %dynamic-slice_bitcast_fusion.3), channel_id=1, source_target_pairs={{0,8},{2,10},{4,12},{6,14},{8,0},{10,2},{12,4},{14,6},{1,9},{3,11}... | collective-permute-start | bytes 4718600 | tf_op jit(solution)/shard_map/ppermute | solution.py:36
  534.5 127.4 %collective-permute-start.10 = (bf16[1,384,2048]{2,1,0:T(8,128)(2,1)}, bf16[1,384,2048]{2,1,0:T(8,128)(2,1)}, u32[]{:S(2)}, u32[]{:S(2)}) collective-permute-start(bf16[1,384,2048]{2,1,0:T(8,128)(2,1)} %dynamic-slice_bitcast_fusion.1), channel_id=1, source_target_pairs={{0,8},{2,10},{4,12},{6,14},{8,0},{10,2},{12,4},{14,6},{1,9},{3,11}... | collective-permute-start | bytes 4718600 | tf_op jit(solution)/shard_map/ppermute | solution.py:36
  671.1 4.2 copy-start.1
  (3 other events, 7.2 us)
Sparse Core Ops, SparseCore 0:
  167.0 335.2 all-reduce.2
